TPU v7x, 32 devices: a whole 2x2x4 slice. The times are simulated.
32 devices in a mesh: fsdp: 8 (over z, x), tp: 4 (over y, core).
Axes of the slice: x: 2, y: 2, z: 4, core: 2. Of those that a mesh axis runs over, the one named last changes fastest.
Arguments:
- history: bfloat16 [8, 4096, 2048], P(None, 'fsdp'), may hold values from -6 to 6
- mix_in: float32 [4096, 32], P('fsdp'), may hold values from -2.4 to 2.4
- doc_positions: int32 [4096], P('fsdp'), may hold values from 0 to 2047, as said below
- gain_q: bfloat16 [2048], P('fsdp'), may hold values from 0.25 to 1.75
- gain_k: bfloat16 [2048], P('fsdp'), may hold values from 0.25 to 1.75
- gain_v: bfloat16 [2048], P('fsdp'), may hold values from 0.25 to 1.75
- gain_mlp: bfloat16 [2048], P('fsdp'), may hold values from 0.25 to 1.75
- gain_mix: bfloat16 [2048], P('fsdp'), may hold values from 0.25 to 1.75
- w_query: bfloat16 [2048, 2048], P('fsdp', 'tp'), may hold values from -0.125 to 0.125
- w_key: bfloat16 [2048, 2048], P('fsdp', 'tp'), may hold values from -0.125 to 0.125
- w_value: bfloat16 [2048, 2048], P('fsdp', 'tp'), may hold values from -0.125 to 0.125
- w_attn_out: bfloat16 [2048, 2048], P('fsdp', 'tp'), may hold values from -1 to 1
- w_mlp_in: bfloat16 [2048, 8192], P('fsdp', 'tp'), may hold values from -0.125 to 0.125
- w_mlp_out: bfloat16 [2048, 8192], P('fsdp', 'tp'), may hold values from -0.0625 to 0.0625
- w_mix_in: bfloat16 [2048, 36], P('fsdp'), may hold values from -0.125 to 0.125
- w_mix_out: bfloat16 [36, 36], replicated, may hold values from -1 to 1
- out_grad: bfloat16 [4096, 2048], P('fsdp'), may hold values from -6 to 6
- next_grad: float32 [4096, 36], P('fsdp'), may hold values from -6 to 6
Outputs:
- block_out: bfloat16 [4096, 2048], P('fsdp')
- next_mix: float32 [4096, 36], P('fsdp')
- history_grad: bfloat16 [8, 4096, 2048], P(None, 'fsdp')
- mix_grad: float32 [4096, 32], P('fsdp')
- grad_gain_q: float32 [2048], P('fsdp')
- grad_gain_k: float32 [2048], P('fsdp')
- grad_gain_v: float32 [2048], P('fsdp')
- grad_gain_mlp: float32 [2048], P('fsdp')
- grad_gain_mix: float32 [2048], P('fsdp')
- grad_w_query: float32 [2048, 2048], P('fsdp', 'tp')
- grad_w_key: float32 [2048, 2048], P('fsdp', 'tp')
- grad_w_value: float32 [2048, 2048], P('fsdp', 'tp')
- grad_w_attn_out: float32 [2048, 2048], P('fsdp', 'tp')
- grad_w_mlp_in: float32 [2048, 8192], P('fsdp', 'tp')
- grad_w_mlp_out: float32 [2048, 8192], P('fsdp', 'tp')
- grad_w_mix_in: float32 [2048, 36], P('fsdp')
- grad_w_mix_out: float32 [36, 36], replicated
Inputs may be any that keep to these rules, and one draw needn't show every extreme that they name: `doc_positions`: documents are runs of consecutive tokens; every multiple of 2048 begins one, so no document crosses a sequence; the first sequence is a single document.
All inputs are finite; a program needn't handle non-finite values.
Results may differ from a plain program's by a relative error of at most 0.017.
Values may be sent and summed in bfloat16 or wider, within the bound.
A program may use at most 256 MiB of HBM per device.

v0:
```python
import math

import jax
import jax.numpy as jnp
from jax import lax
from jax.sharding import PartitionSpec as P

HD = 128
ROT = 32
WAYS = 4
DEPTH = 8
SEQLEN = 2048


EPS = 1e-05
NEG = -1e30


def shifted(shard, axis, by):
    length = lax.axis_size(axis)
    return lax.ppermute(shard, axis, [(i, (i + by) % length) for i in range(length)])


def layer_norm(values, gain_vec):
    centre = values - jnp.mean(values, -1, keepdims=True)
    return centre * lax.rsqrt(jnp.mean(centre * centre, -1, keepdims=True) + EPS) * gain_vec


def rope_turn(values, positions, turn_sign):
    half_rot = ROT // 2
    frequency = 10000.0 ** (-2.0 * jnp.arange(half_rot, dtype=jnp.float32) / ROT)
    angle_table = positions.astype(jnp.float32)[:, None] * frequency[None, :]
    cosine = jnp.cos(angle_table)[:, None, :]
    sine_part = turn_sign * jnp.sin(angle_table)[:, None, :]
    lead_half = values[..., :half_rot]
    second = values[..., half_rot:ROT]
    return jnp.concatenate(
        [
            lead_half * cosine - second * sine_part,
            second * cosine + lead_half * sine_part,
            values[..., ROT:],
        ],
        -1,
    )


def gelu_exact(values):
    return jax.nn.gelu(values, approximate=False)


def mix_network(block_val, gain_vec, mat_first, mat_second):
    highest = lax.Precision.HIGHEST
    hidden = gelu_exact(jnp.dot(layer_norm(block_val, gain_vec), mat_first, precision=highest))
    return jnp.dot(hidden, mat_second, precision=highest)


def head_total(partial_value):
    return lax.psum(partial_value, "tp")


def contract_rows(left, right):
    return lax.dot_general(
        left, right, (((0,), (0,)), ((), ())), preferred_element_type=jnp.float32
    )


def contract_cols(left, right):
    return lax.dot_general(
        left, right, (((1,), (1,)), ((), ())), preferred_element_type=jnp.float32
    )


def visible_keys(query_index, positions, key_start, row_count):
    key_index = key_start + jnp.arange(row_count, dtype=jnp.int32)
    return (key_index[None, :] <= query_index[:, None]) & (
        key_index[None, :] >= (query_index - positions)[:, None]
    )


def attend_piece(soft_stats, queries, key_rows, value_rows, visible):
    top_old, row_total, accumulated = soft_stats
    head_scale = 1.0 / math.sqrt(HD)
    scores = (
        jnp.einsum("qhd,khd->hqk", queries, key_rows, preferred_element_type=jnp.float32)
        * head_scale
    )
    key_mask = visible[None]
    row_top = jnp.maximum(top_old, jnp.max(jnp.where(key_mask, scores, NEG), -1))
    weights = jnp.where(key_mask, jnp.exp(scores - row_top[..., None]), 0.0)
    shrink = jnp.exp(top_old - row_top)
    row_total = row_total * shrink + jnp.sum(weights, -1)
    accumulated = accumulated * shrink.T[:, :, None] + jnp.einsum(
        "hqk,khd->qhd", weights.astype(jnp.bfloat16), value_rows, preferred_element_type=jnp.float32
    )
    return (row_top, row_total, accumulated)


def attend_back(queries, key_rows, value_rows, visible, grad_out, log_total, delta):
    head_scale = 1.0 / math.sqrt(HD)
    scores = (
        jnp.einsum("qhd,khd->hqk", queries, key_rows, preferred_element_type=jnp.float32)
        * head_scale
    )
    probabilities = jnp.where(visible[None], jnp.exp(scores - log_total[..., None]), 0.0)
    grad_probs = jnp.einsum(
        "qhd,khd->hqk", grad_out, value_rows, preferred_element_type=jnp.float32
    )
    grad_scores = (probabilities * (grad_probs - delta[..., None])).astype(jnp.bfloat16)
    grad_query = (
        jnp.einsum("hqk,khd->qhd", grad_scores, key_rows, preferred_element_type=jnp.float32)
        * head_scale
    )
    grad_key = (
        jnp.einsum("hqk,qhd->khd", grad_scores, queries, preferred_element_type=jnp.float32)
        * head_scale
    )
    grad_value = jnp.einsum(
        "hqk,qhd->khd",
        probabilities.astype(jnp.bfloat16),
        grad_out,
        preferred_element_type=jnp.float32,
    )
    return (grad_query, grad_key, grad_value)


def forward_pass(inputs):
    (
        history,
        mix_in,
        doc_positions,
        gain_q,
        gain_k,
        gain_v,
        gain_mlp,
        gain_mix,
        w_query,
        w_key,
        w_value,
        w_attn_out,
        w_mlp_in,
        w_mlp_out,
        w_mix_in,
        w_mix_out,
    ) = inputs
    tokens = history.shape[1]
    model_width = history.shape[2]
    head_count = w_query.shape[1] // HD
    group_size = SEQLEN // tokens
    wq_all, wk_all, wv_all, wo_all, gq_all, gk_all, gv_all = (
        lax.all_gather(w_query, "fsdp", axis=0, tiled=True),
        lax.all_gather(w_key, "fsdp", axis=0, tiled=True),
        lax.all_gather(w_value, "fsdp", axis=0, tiled=True),
        lax.all_gather(w_attn_out, "fsdp", axis=0, tiled=True),
        lax.all_gather(gain_q, "fsdp", axis=0, tiled=True),
        lax.all_gather(gain_k, "fsdp", axis=0, tiled=True),
        lax.all_gather(gain_v, "fsdp", axis=0, tiled=True),
    )
    mixing = mix_in.reshape(tokens, WAYS, DEPTH)
    ways = jnp.zeros((WAYS, tokens, model_width), jnp.float32)
    for depth_index in range(DEPTH):
        ways = (
            ways
            + mixing[:, :, depth_index].T[:, :, None]
            * history[depth_index].astype(jnp.float32)[None]
        )
    gq_f = gq_all.astype(jnp.float32)
    gk_f = gk_all.astype(jnp.float32)
    gv_f = gv_all.astype(jnp.float32)
    q_in = layer_norm(ways[0], gq_f).astype(jnp.bfloat16)
    k_in = layer_norm(ways[1], gk_f).astype(jnp.bfloat16)
    v_in = layer_norm(ways[2], gv_f).astype(jnp.bfloat16)
    queries = rope_turn(
        jnp.dot(q_in, wq_all, preferred_element_type=jnp.float32).reshape(tokens, head_count, HD),
        doc_positions,
        1.0,
    ).astype(jnp.bfloat16)
    key_rows = rope_turn(
        jnp.dot(k_in, wk_all, preferred_element_type=jnp.float32).reshape(tokens, head_count, HD),
        doc_positions,
        1.0,
    ).astype(jnp.bfloat16)
    value_rows = (
        jnp.dot(v_in, wv_all, preferred_element_type=jnp.float32)
        .astype(jnp.bfloat16)
        .reshape(tokens, head_count, HD)
    )
    device_count = lax.axis_size("fsdp")
    own_index = lax.axis_index("fsdp")
    local_rows = jnp.arange(tokens, dtype=jnp.int32)
    query_index = own_index * tokens + local_rows
    soft_stats = (
        jnp.full((head_count, tokens), NEG, jnp.float32),
        jnp.zeros((head_count, tokens), jnp.float32),
        jnp.zeros((tokens, head_count, HD), jnp.float32),
    )
    soft_stats = attend_piece(
        soft_stats,
        queries,
        key_rows,
        value_rows,
        visible_keys(query_index, doc_positions, own_index * tokens, tokens),
    )

    def walk_queries(walk_step, carry):
        moved = shifted((carry[0], carry[1], carry[2], carry[3], carry[4]), "fsdp", -1)
        travel_queries, travel_positions, top_now, total_now, acc_now = moved
        anchor = (own_index + walk_step) % device_count
        travel_index = anchor * tokens + local_rows
        visible_now = visible_keys(
            travel_index, travel_positions.astype(jnp.int32), own_index * tokens, tokens
        )
        top_now, total_now, acc_now = attend_piece(
            (top_now, total_now, acc_now),
            travel_queries.astype(jnp.bfloat16),
            key_rows,
            value_rows,
            visible_now,
        )
        return (travel_queries, travel_positions, top_now, total_now, acc_now)

    start_carry = (
        queries.astype(jnp.float32),
        doc_positions.astype(jnp.float32),
        soft_stats[0],
        soft_stats[1],
        soft_stats[2],
    )
    walked = lax.fori_loop(1, group_size, walk_queries, start_carry)
    row_top, row_total, accumulated = shifted(
        (walked[2], walked[3], walked[4]), "fsdp", group_size - 1
    )
    attn_rows = accumulated / row_total.T[:, :, None]
    log_total = row_top + jnp.log(row_total)
    attn_low = attn_rows.reshape(tokens, head_count * HD).astype(jnp.bfloat16)
    residual = ways[3] + head_total(contract_cols(attn_low, wo_all))
    wi_all, wf_all, gm_all, w1_all, gx_all = (
        lax.all_gather(w_mlp_in, "fsdp", axis=0, tiled=True),
        lax.all_gather(w_mlp_out, "fsdp", axis=0, tiled=True),
        lax.all_gather(gain_mlp, "fsdp", axis=0, tiled=True),
        lax.all_gather(w_mix_in, "fsdp", axis=0, tiled=True),
        lax.all_gather(gain_mix, "fsdp", axis=0, tiled=True),
    )
    gm_f = gm_all.astype(jnp.float32)
    mlp_in = layer_norm(residual, gm_f).astype(jnp.bfloat16)
    up_proj = jnp.dot(mlp_in, wi_all, preferred_element_type=jnp.float32)
    act_rows = gelu_exact(up_proj).astype(jnp.bfloat16)
    block_val = residual + head_total(contract_cols(act_rows, wf_all))
    gx_f = gx_all.astype(jnp.float32)
    first_mix = w1_all.astype(jnp.float32)
    second_mix = w_mix_out.astype(jnp.float32)
    next_val = mix_network(block_val, gx_f, first_mix, second_mix)
    return {
        "ways": ways,
        "q_in": q_in,
        "k_in": k_in,
        "v_in": v_in,
        "queries": queries,
        "key_rows": key_rows,
        "value_rows": value_rows,
        "attn_rows": attn_rows,
        "log_total": log_total,
        "attn_low": attn_low,
        "residual": residual,
        "mlp_in": mlp_in,
        "up_proj": up_proj,
        "act_rows": act_rows,
        "block_val": block_val,
        "next_val": next_val,
        "wq_all": wq_all,
        "wk_all": wk_all,
        "wv_all": wv_all,
        "wo_all": wo_all,
        "gq_f": gq_f,
        "gk_f": gk_f,
        "gv_f": gv_f,
        "wi_all": wi_all,
        "wf_all": wf_all,
        "gm_f": gm_f,
        "gx_f": gx_f,
        "first_mix": first_mix,
        "second_mix": second_mix,
    }


def local(
    history,
    mix_in,
    doc_positions,
    gain_q,
    gain_k,
    gain_v,
    gain_mlp,
    gain_mix,
    w_query,
    w_key,
    w_value,
    w_attn_out,
    w_mlp_in,
    w_mlp_out,
    w_mix_in,
    w_mix_out,
    out_grad,
    next_grad,
):
    inputs = (
        history,
        mix_in,
        doc_positions,
        gain_q,
        gain_k,
        gain_v,
        gain_mlp,
        gain_mix,
        w_query,
        w_key,
        w_value,
        w_attn_out,
        w_mlp_in,
        w_mlp_out,
        w_mix_in,
        w_mix_out,
    )
    first_pass = forward_pass(inputs)
    again_inputs = lax.optimization_barrier((inputs, first_pass["block_val"]))[0]
    saved_pass = forward_pass(again_inputs)
    tokens = history.shape[1]
    head_count = w_query.shape[1] // HD
    group_size = SEQLEN // tokens
    mixing = mix_in.reshape(tokens, WAYS, DEPTH)
    next_val, mix_pullback = jax.vjp(
        mix_network,
        saved_pass["block_val"],
        saved_pass["gx_f"],
        saved_pass["first_mix"],
        saved_pass["second_mix"],
    )
    g_block_mix, g_gain_mix, g_mix_first, g_mix_second = mix_pullback(next_grad)
    g_block = out_grad.astype(jnp.float32) + g_block_mix
    g_block_low = g_block.astype(jnp.bfloat16)
    g_act = jnp.dot(g_block_low, saved_pass["wf_all"], preferred_element_type=jnp.float32)
    gelu_pullback = jax.vjp(gelu_exact, saved_pass["up_proj"])[1]
    g_up = gelu_pullback(g_act)[0].astype(jnp.bfloat16)
    grad_mlp_out = contract_rows(g_block_low, saved_pass["act_rows"])
    grad_mlp_in = contract_rows(saved_pass["mlp_in"], g_up)
    g_mlp_in = lax.psum(contract_cols(g_up, saved_pass["wi_all"]), "tp")
    norm_pullback = jax.vjp(layer_norm, saved_pass["residual"], saved_pass["gm_f"])[1]
    g_res_norm, g_gain_mlp = norm_pullback(g_mlp_in)
    g_res = g_block + g_res_norm
    mlp_sums = (
        lax.psum_scatter(grad_mlp_in, "fsdp", scatter_dimension=0, tiled=True),
        lax.psum_scatter(grad_mlp_out, "fsdp", scatter_dimension=0, tiled=True),
        lax.psum_scatter(g_gain_mlp, "fsdp", scatter_dimension=0, tiled=True),
        lax.psum_scatter(g_mix_first, "fsdp", scatter_dimension=0, tiled=True),
        lax.psum_scatter(g_gain_mix, "fsdp", scatter_dimension=0, tiled=True),
    )
    g_res_low = g_res.astype(jnp.bfloat16)
    grad_attn_out = contract_rows(g_res_low, saved_pass["attn_low"])
    g_attn = (
        jnp.dot(g_res_low, saved_pass["wo_all"], preferred_element_type=jnp.float32)
        .astype(jnp.bfloat16)
        .reshape(tokens, head_count, HD)
    )
    delta = jnp.sum(g_attn.astype(jnp.float32) * saved_pass["attn_rows"], -1).T
    queries = saved_pass["queries"]
    key_rows = saved_pass["key_rows"]
    value_rows = saved_pass["value_rows"]
    log_total = saved_pass["log_total"]
    device_count = lax.axis_size("fsdp")
    own_index = lax.axis_index("fsdp")
    local_rows = jnp.arange(tokens, dtype=jnp.int32)
    query_index = own_index * tokens + local_rows
    own_visible = visible_keys(query_index, doc_positions, own_index * tokens, tokens)
    g_query, g_key, g_value = attend_back(
        queries, key_rows, value_rows, own_visible, g_attn, log_total, delta
    )

    def walk_back(walk_step, carry):
        moved = shifted((carry[0], carry[1], carry[2], carry[3], carry[4], carry[5]), "fsdp", -1)
        travel_queries, travel_grads, travel_lse, travel_delta, travel_positions, acc_query = moved
        acc_key, acc_value = (carry[6], carry[7])
        anchor = (own_index + walk_step) % device_count
        travel_index = anchor * tokens + local_rows
        visible_now = visible_keys(
            travel_index, travel_positions.astype(jnp.int32), own_index * tokens, tokens
        )
        part_query, part_key, part_value = attend_back(
            travel_queries.astype(jnp.bfloat16),
            key_rows,
            value_rows,
            visible_now,
            travel_grads.astype(jnp.bfloat16),
            travel_lse,
            travel_delta,
        )
        return (
            travel_queries,
            travel_grads,
            travel_lse,
            travel_delta,
            travel_positions,
            acc_query + part_query,
            acc_key + part_key,
            acc_value + part_value,
        )

    back_carry = (
        queries.astype(jnp.float32),
        g_attn.astype(jnp.float32),
        log_total,
        delta,
        doc_positions.astype(jnp.float32),
        g_query,
        g_key,
        g_value,
    )
    walked = lax.fori_loop(1, group_size, walk_back, back_carry)
    g_query = shifted(walked[5], "fsdp", group_size - 1)
    g_key = walked[6]
    g_value = walked[7]
    g_q_raw = (
        rope_turn(g_query, doc_positions, -1.0)
        .reshape(tokens, head_count * HD)
        .astype(jnp.bfloat16)
    )
    g_k_raw = (
        rope_turn(g_key, doc_positions, -1.0).reshape(tokens, head_count * HD).astype(jnp.bfloat16)
    )
    g_v_raw = g_value.reshape(tokens, head_count * HD).astype(jnp.bfloat16)
    grad_query = contract_rows(saved_pass["q_in"], g_q_raw)
    grad_key = contract_rows(saved_pass["k_in"], g_k_raw)
    grad_value = contract_rows(saved_pass["v_in"], g_v_raw)
    g_q_in, g_k_in, g_v_in = lax.psum(
        (
            contract_cols(g_q_raw, saved_pass["wq_all"]),
            contract_cols(g_k_raw, saved_pass["wk_all"]),
            contract_cols(g_v_raw, saved_pass["wv_all"]),
        ),
        "tp",
    )
    ways = saved_pass["ways"]
    g_way_q, g_gain_q = jax.vjp(layer_norm, ways[0], saved_pass["gq_f"])[1](g_q_in)
    g_way_k, g_gain_k = jax.vjp(layer_norm, ways[1], saved_pass["gk_f"])[1](g_k_in)
    g_way_v, g_gain_v = jax.vjp(layer_norm, ways[2], saved_pass["gv_f"])[1](g_v_in)
    way_grads = [g_way_q, g_way_k, g_way_v, g_res]
    history_parts = []
    for depth_index in range(DEPTH):
        total_grad = mixing[:, 0, depth_index][:, None] * way_grads[0]
        for way_index in range(1, WAYS):
            total_grad = (
                total_grad + mixing[:, way_index, depth_index][:, None] * way_grads[way_index]
            )
        history_parts.append(total_grad.astype(jnp.bfloat16))
    history_grad = jnp.stack(history_parts, 0)
    mix_columns = []
    for way_index in range(WAYS):
        for depth_index in range(DEPTH):
            mix_columns.append(
                jnp.sum(way_grads[way_index] * history[depth_index].astype(jnp.float32), -1)
            )
    mix_grad = jnp.stack(mix_columns, 1)
    attn_sums = (
        lax.psum_scatter(grad_query, "fsdp", scatter_dimension=0, tiled=True),
        lax.psum_scatter(grad_key, "fsdp", scatter_dimension=0, tiled=True),
        lax.psum_scatter(grad_value, "fsdp", scatter_dimension=0, tiled=True),
        lax.psum_scatter(grad_attn_out, "fsdp", scatter_dimension=0, tiled=True),
        lax.psum_scatter(g_gain_q, "fsdp", scatter_dimension=0, tiled=True),
        lax.psum_scatter(g_gain_k, "fsdp", scatter_dimension=0, tiled=True),
        lax.psum_scatter(g_gain_v, "fsdp", scatter_dimension=0, tiled=True),
    )
    grad_mix_out = lax.psum(g_mix_second, "fsdp")
    block_out = first_pass["block_val"].astype(jnp.bfloat16)
    return (
        block_out,
        first_pass["next_val"],
        history_grad,
        mix_grad,
        attn_sums[4],
        attn_sums[5],
        attn_sums[6],
        mlp_sums[2],
        mlp_sums[4],
        attn_sums[0],
        attn_sums[1],
        attn_sums[2],
        attn_sums[3],
        mlp_sums[0],
        mlp_sums[1],
        mlp_sums[3],
        grad_mix_out,
    )


def solution(mesh):
    in_specs = (
        P(None, "fsdp", None),
        P("fsdp", None),
        P("fsdp"),
        P("fsdp"),
        P("fsdp"),
        P("fsdp"),
        P("fsdp"),
        P("fsdp"),
        P("fsdp", "tp"),
        P("fsdp", "tp"),
        P("fsdp", "tp"),
        P("fsdp", "tp"),
        P("fsdp", "tp"),
        P("fsdp", "tp"),
        P("fsdp", None),
        P(),
        P("fsdp", None),
        P("fsdp", None),
    )
    out_specs = (
        P("fsdp", None),
        P("fsdp", None),
        P(None, "fsdp", None),
        P("fsdp", None),
        P("fsdp"),
        P("fsdp"),
        P("fsdp"),
        P("fsdp"),
        P("fsdp"),
        P("fsdp", "tp"),
        P("fsdp", "tp"),
        P("fsdp", "tp"),
        P("fsdp", "tp"),
        P("fsdp", "tp"),
        P("fsdp", "tp"),
        P("fsdp", None),
        P(),
    )
    return jax.shard_map(local, mesh=mesh, in_specs=in_specs, out_specs=out_specs, check_vma=False)
```

profile of v0, /device:TPU:0, one launch (start us, length us, event | category | flops | bytes accessed | tf_op | source)
XLA Modules:
  0.0 3204.0 jit_solution(6305266001976689446)
XLA Ops:
  125.1 37.2 %all-gather.27.cloned.1.call-done = bf16[2048,512]{1,0:T(8,128)(2,1)} async-done(((bf16[256,512]{1,0:T(8,128)(2,1)}), bf16[2048,512]{1,0:T(8,128)(2,1)}) %all-gather.27.cloned.1.call-update) | async-done | bytes 2097168 | tf_op jit(solution)/shard_map/all_gather | solution.py:152
  172.5 149.0 %while.78 = (s32[]{:T(128)}, bf16[512,4,128]{2,0,1:T(8,128)(2,1)}, f32[512]{0:T(512)S(1)}, f32[4,512]{1,0:T(4,128)S(1)}, f32[4,512]{1,0:T(4,128)S(1)}, /*index=5...) while((s32[]{:T(128)}, bf16[512,4,128]{2,0,1:T(8,128)(2,1)}, ...), condition=%wide.region_11.12_spmd.clone, body=%wide.region_8.11_spmd.clone.sunk | while | flops 549724672 | bytes 24848868 | solution.py:228
  324.3 44.9 %collective-permute-done.17 = f32[4,512]{1,0:T(4,128)S(1)} collective-permute-done((f32[4,512]{1,0:T(4,128)S(1)}, f32[4,512]{1,0:T(4,128)S(1)}, u32[]{:S(2)}, u32[]{:S(2)}) %collective-permute-start.17) | collective-permute-done | bytes 8224 | tf_op jit(solution)/shard_map/ppermute | solution.py:21
  392.1 65.6 %all-reduce.14.cloned.1.call-done = f32[512,2048]{1,0:T(8,128)} async-done(((f32[512,2048]{1,0:T(8,128)}), f32[512,2048]{1,0:T(8,128)}) %all-reduce.14.cloned.1.call-update) | async-done | bytes 4194320 | tf_op jit(solution)/shard_map/psum | solution.py:58
  464.3 120.8 %all-gather.31.cloned.1.call-done = bf16[2048,2048]{1,0:T(8,128)(2,1)} async-done(((bf16[256,2048]{1,0:T(8,128)(2,1)}), bf16[2048,2048]{1,0:T(8,128)(2,1)}) %all-gather.31.cloned.1.call-update) | async-done | bytes 8388624 | tf_op jit(solution)/shard_map/all_gather | solution.py:237
  585.0 125.5 %all-gather.33.cloned.1.call-done = bf16[2048,2048]{1,0:T(8,128)(2,1)} async-done(((bf16[256,2048]{1,0:T(8,128)(2,1)}), bf16[2048,2048]{1,0:T(8,128)(2,1)}) %all-gather.33.cloned.1.call-update) | async-done | bytes 8388624 | tf_op jit(solution)/shard_map/all_gather | solution.py:238
  734.9 83.8 %all-reduce.16.cloned.1.call-done = f32[512,2048]{1,0:T(8,128)} async-done(((f32[512,2048]{1,0:T(8,128)}), f32[512,2048]{1,0:T(8,128)}) %all-reduce.16.cloned.1.call-update) | async-done | bytes 4194320 | tf_op jit(solution)/shard_map/psum | solution.py:58
  937.2 37.5 %all-gather.39.cloned.1.call-done = bf16[2048,512]{1,0:T(8,128)(2,1)} async-done(((bf16[256,512]{1,0:T(8,128)(2,1)}), bf16[2048,512]{1,0:T(8,128)(2,1)}) %all-gather.39.cloned.1.call-update) | async-done | bytes 2097168 | tf_op jit(solution)/shard_map/all_gather | solution.py:152
  986.7 146.0 %while.79 = (s32[]{:T(128)}, bf16[512,4,128]{2,0,1:T(8,128)(2,1)S(1)}, f32[512]{0:T(512)S(1)}, f32[4,512]{1,0:T(4,128)S(1)}, f32[4,512]{1,0:T(4,128)S(1)}, /*ind...) while((s32[]{:T(128)}, ...), condition=%wide.region_29.30_spmd.clone, body=%wide.region_26.29_spmd.clone.sunk | while | flops 549724672 | bytes 26946048 | solution.py:228
  1136.3 43.9 %collective-permute-done.19 = f32[4,512]{1,0:T(4,128)S(1)} collective-permute-done((f32[4,512]{1,0:T(4,128)S(1)}, f32[4,512]{1,0:T(4,128)S(1)}, u32[]{:S(2)}, u32[]{:S(2)}) %collective-permute-start.19) | collective-permute-done | bytes 8224 | tf_op jit(solution)/shard_map/ppermute | solution.py:21
  1204.0 65.5 %all-reduce.18.cloned.1.call-done = f32[512,2048]{1,0:T(8,128)} async-done(((f32[512,2048]{1,0:T(8,128)}), f32[512,2048]{1,0:T(8,128)}) %all-reduce.18.cloned.1.call-update) | async-done | bytes 4194320 | tf_op jit(solution)/shard_map/psum | solution.py:58
  1276.0 120.8 %all-gather.43.cloned.1.call-done = bf16[2048,2048]{1,0:T(8,128)(2,1)} async-done(((bf16[256,2048]{1,0:T(8,128)(2,1)}), bf16[2048,2048]{1,0:T(8,128)(2,1)}) %all-gather.43.cloned.1.call-update) | async-done | bytes 8388624 | tf_op jit(solution)/shard_map/all_gather | solution.py:237
  1415.8 106.3 %all-gather.45.cloned.1.call-done = bf16[2048,2048]{1,0:T(8,128)(2,1)} async-done(((bf16[256,2048]{1,0:T(8,128)(2,1)}), bf16[2048,2048]{1,0:T(8,128)(2,1)}) %all-gather.45.cloned.1.call-update) | async-done | bytes 8388624 | tf_op jit(solution)/shard_map/all_gather | solution.py:238
  1580.6 34.8 %all-reduce.20.cloned.1.call-done = f32[512,2048]{1,0:T(8,128)} async-done(((f32[512,2048]{1,0:T(8,128)}), f32[512,2048]{1,0:T(8,128)}) %all-reduce.20.cloned.1.call-update) | async-done | bytes 4194320 | tf_op jit(solution)/shard_map/psum | solution.py:58
  1653.3 80.0 %all-reduce.22.cloned.1.call-done = f32[512,2048]{1,0:T(8,128)} async-done(((f32[512,2048]{1,0:T(8,128)}), f32[512,2048]{1,0:T(8,128)}) %all-reduce.22.cloned.1.call-update) | async-done | bytes 4194320 | tf_op jit(solution)/shard_map/psum | solution.py:345
  1758.2 156.4 %while.80 = (s32[]{:T(128)}, bf16[512,4,128]{2,0,1:T(8,128)(2,1)}, bf16[512,4,128]{2,0,1:T(8,128)(2,1)}, f32[4,512]{1,0:T(4,128)S(1)}, f32[4,512]{1,0:T(4,128)S(...) while((s32[]{:T(128)}, bf16[512,4,128]{2,0,1:T(8,128)(2,1)}, ...), condition=%wide.region_43.44_spmd.clone, body=%wide.region_42.43_spmd.clone.sunk | while | flops 1354762752 | bytes 50743924 | solution.py:416
  1925.6 35.8 %collective-permute-done.21 = f32[512,4,128]{0,2,1:T(8,128)} collective-permute-done((f32[512,4,128]{0,2,1:T(8,128)}, f32[512,4,128]{0,2,1:T(8,128)}, u32[]{:S(2)}, u32[]{:S(2)}) %collective-permute-start.21) | collective-permute-done | bytes 1048608 | tf_op jit(solution)/shard_map/ppermute | solution.py:21
  2085.1 105.1 %all-reduce.24.cloned.1.call-done = (f32[512,2048]{1,0:T(8,128)}, f32[512,2048]{1,0:T(8,128)}, f32[512,2048]{1,0:T(8,128)}) async-done(((f32[512,2048]{1,0:T(8,128)}, f32[512,2048]{1,0:T(8,128)}, f32[512,2048]{1,0:T(8,128)}), (f32[512,2048]{1,0:T(8,128)}, f32[512,2048]{1,0:T(8,128)}, f32[512,2048]{1,0:T(8,128)})) %all-reduce.24.cloned.1.call-update) | async-done | bytes 12582928 | tf_op jit(solution)/shard_map/psum | solution.py:432
  2200.1 38.1 %all-reduce.5 = (f32[2048]{0:T(1024)S(1)}, f32[2048]{0:T(1024)S(1)}, f32[2048]{0:T(1024)S(1)}, f32[2048]{0:T(1024)S(1)}, f32[2048]{0:T(1024)S(1)}, /*index=5*/f32[36,36]{1,0:T(8,128)}) all-reduce(f32[2048]{0:T(1024)S(1)} %get-tuple-element.1087, f32[2048]{0:T(1024)S(1)} %get-tuple-element.1085, ...), channel_id=2, replica_groups=mesh['fsdp'=8,'tp'=4] {'fsdp'}, use_global_device_ids=true, to_apply=%region_86.87.clone | all-reduce | flops 11536 | bytes 92288
  2348.8 91.9 %reduce-scatter.14.cloned.1.call-done = f32[256,512]{1,0:T(8,128)} async-done(((f32[2048,512]{1,0:T(8,128)}), f32[256,512]{1,0:T(8,128)}) %reduce-scatter.14.cloned.1.call-update) | async-done | bytes 524304 | tf_op jit(solution)/shard_map/reduce_scatter | solution.py:465
  2440.7 92.3 %reduce-scatter.8.cloned.1.call-done = f32[256,512]{1,0:T(8,128)} async-done(((f32[2048,512]{1,0:T(8,128)}), f32[256,512]{1,0:T(8,128)}) %reduce-scatter.8.cloned.1.call-update) | async-done | bytes 524304 | tf_op jit(solution)/shard_map/reduce_scatter | solution.py:462
  2533.0 91.9 %reduce-scatter.10.cloned.1.call-done = f32[256,512]{1,0:T(8,128)} async-done(((f32[2048,512]{1,0:T(8,128)}), f32[256,512]{1,0:T(8,128)}) %reduce-scatter.10.cloned.1.call-update) | async-done | bytes 524304 | tf_op jit(solution)/shard_map/reduce_scatter | solution.py:463
  2624.8 286.4 %reduce-scatter.16.cloned.1.call-done = f32[256,2048]{1,0:T(8,128)} async-done(((f32[2048,2048]{1,0:T(8,128)}), f32[256,2048]{1,0:T(8,128)}) %reduce-scatter.16.cloned.1.call-update) | async-done | bytes 2097168 | tf_op jit(solution)/shard_map/reduce_scatter | solution.py:350
  2911.2 286.0 %reduce-scatter.18.cloned.1.call-done = f32[256,2048]{1,0:T(8,128)} async-done(((f32[2048,2048]{1,0:T(8,128)}), f32[256,2048]{1,0:T(8,128)}) %reduce-scatter.18.cloned.1.call-update) | async-done | bytes 2097168 | tf_op jit(solution)/shard_map/reduce_scatter | solution.py:351
  (713 shorter events, 1191.7 us)
Async XLA Ops:
  7.2 100.8 %all-gather.23.cloned.1.call-start = ((), (), s32[]{:S(2)}) async-start(), calls=%async_computation.7 | async-start | bytes 2359296 | tf_op jit(solution)/shard_map/all_gather | solution.py:150
  7.9 104.4 %all-gather.25.cloned.1.call-start = ((), (), s32[]{:S(2)}) async-start(), calls=%async_computation.8 | async-start | bytes 2359296 | tf_op jit(solution)/shard_map/all_gather | solution.py:151
  8.7 153.5 %all-gather.27.cloned.1.call-start = ((), (), s32[]{:S(2)}) async-start(), calls=%async_computation.9 | async-start | bytes 2359296 | tf_op jit(solution)/shard_map/all_gather | solution.py:152
  9.4 359.9 %all-gather.29.cloned.1.call-start = ((), (), s32[]{:S(2)}) async-start(), calls=%async_computation.10 | async-start | bytes 2359296 | tf_op jit(solution)/shard_map/all_gather | solution.py:153
  10.0 447.7 %all-reduce.14.cloned.1.call-start = ((), (), s32[]{:S(2)}) async-start(), calls=%async_computation.11 | async-start | bytes 8388608 | tf_op jit(solution)/shard_map/psum | solution.py:58
  374.2 210.8 %all-gather.31.cloned.1.call-start = ((), (), s32[]{:S(2)}) async-start(), calls=%async_computation.12 | async-start | bytes 9437184 | tf_op jit(solution)/shard_map/all_gather | solution.py:237
  374.8 335.7 %all-gather.33.cloned.1.call-start = ((), (), s32[]{:S(2)}) async-start(), calls=%async_computation.13 | async-start | bytes 9437184 | tf_op jit(solution)/shard_map/all_gather | solution.py:238
  375.5 443.2 %all-reduce.16.cloned.1.call-start = ((), (), s32[]{:S(2)}) async-start(), calls=%async_computation.14 | async-start | bytes 8388608 | tf_op jit(solution)/shard_map/psum | solution.py:58
  734.9 182.6 %all-gather.37.cloned.1.call-start = ((), (), s32[]{:S(2)}) async-start(), calls=%async_computation.16 | async-start | bytes 2359296 | tf_op jit(solution)/shard_map/all_gather | solution.py:151
  825.8 148.9 %all-gather.39.cloned.1.call-start = ((), (), s32[]{:S(2)}) async-start(), calls=%async_computation.17 | async-start | bytes 2359296 | tf_op jit(solution)/shard_map/all_gather | solution.py:152
  841.5 339.9 %all-gather.41.cloned.1.call-start = ((), (), s32[]{:S(2)}) async-start(), calls=%async_computation.18 | async-start | bytes 2359296 | tf_op jit(solution)/shard_map/all_gather | solution.py:153
  917.2 352.3 %all-reduce.18.cloned.1.call-start = ((), (), s32[]{:S(2)}) async-start(), calls=%async_computation.19 | async-start | bytes 8388608 | tf_op jit(solution)/shard_map/psum | solution.py:58
  1186.5 210.3 %all-gather.43.cloned.1.call-start = ((), (), s32[]{:S(2)}) async-start(), calls=%async_computation.20 | async-start | bytes 9437184 | tf_op jit(solution)/shard_map/all_gather | solution.py:237
  1187.1 335.1 %all-gather.45.cloned.1.call-start = ((), (), s32[]{:S(2)}) async-start(), calls=%async_computation.21 | async-start | bytes 9437184 | tf_op jit(solution)/shard_map/all_gather | solution.py:238
  1187.6 427.8 %all-reduce.20.cloned.1.call-start = ((), (), s32[]{:S(2)}) async-start(), calls=%async_computation.22 | async-start | bytes 8388608 | tf_op jit(solution)/shard_map/psum | solution.py:58
  1531.6 201.7 %all-reduce.22.cloned.1.call-start = ((), (), s32[]{:S(2)}) async-start(), calls=%async_computation.23 | async-start | bytes 8388608 | tf_op jit(solution)/shard_map/psum | solution.py:345
  1647.5 542.6 %all-reduce.24.cloned.1.call-start = ((), (), s32[]{:S(2)}) async-start(), calls=%async_computation.31 | async-start | bytes 25165824 | tf_op jit(solution)/shard_map/psum | solution.py:432
  1970.4 346.9 %reduce-scatter.20.cloned.1.call-start = ((), (), s32[]{:S(2)}) async-start(), calls=%async_computation.30 | async-start | bytes 368640 | tf_op jit(solution)/shard_map/reduce_scatter | solution.py:353
  1977.3 371.5 %reduce-scatter.12.cloned.1.call-start = ((), (), s32[]{:S(2)}) async-start(), calls=%async_computation.26 | async-start | bytes 4718592 | tf_op jit(solution)/shard_map/reduce_scatter | solution.py:464
  1983.1 457.6 %reduce-scatter.14.cloned.1.call-start = ((), (), s32[]{:S(2)}) async-start(), calls=%async_computation.27 | async-start | bytes 4718592 | tf_op jit(solution)/shard_map/reduce_scatter | solution.py:465
  1989.7 543.3 %reduce-scatter.8.cloned.1.call-start = ((), (), s32[]{:S(2)}) async-start(), calls=%async_computation.24 | async-start | bytes 4718592 | tf_op jit(solution)/shard_map/reduce_scatter | solution.py:462
  1996.1 628.7 %reduce-scatter.10.cloned.1.call-start = ((), (), s32[]{:S(2)}) async-start(), calls=%async_computation.25 | async-start | bytes 4718592 | tf_op jit(solution)/shard_map/reduce_scatter | solution.py:463
  2002.5 908.8 %reduce-scatter.16.cloned.1.call-start = ((), (), s32[]{:S(2)}) async-start(), calls=%async_computation.28 | async-start | bytes 18874368 | tf_op jit(solution)/shard_map/reduce_scatter | solution.py:350
  2014.8 1182.5 %reduce-scatter.18.cloned.1.call-start = ((), (), s32[]{:S(2)}) async-start(), calls=%async_computation.29 | async-start | bytes 18874368 | tf_op jit(solution)/shard_map/reduce_scatter | solution.py:351
  (170 other events, 4923.5 us)
Sparse Core Ops, SparseCore 0:
  10.2 52.1 all-gather.22
  64.4 47.8 all-gather.24
  114.4 47.7 all-gather.26
  164.2 92.2 all-gather.28
  374.3 83.3 all-reduce.13
  459.9 125.0 all-gather.30
  587.4 123.0 all-gather.32
  735.0 83.6 all-reduce.15
  825.4 49.4 all-gather.36
  926.3 48.3 all-gather.38
  976.7 64.4 all-gather.40
  1186.6 82.8 all-reduce.17
  1271.7 125.0 all-gather.42
  1399.0 123.0 all-gather.44
  1531.7 83.6 all-reduce.19
  1647.7 85.6 all-reduce.21
  1970.5 219.5 all-reduce.23
  2194.4 62.9 reduce-scatter.19
  2261.8 86.9 reduce-scatter.11
  2353.0 87.6 reduce-scatter.13
  2445.3 87.6 reduce-scatter.7
  2537.2 87.5 reduce-scatter.9
  2629.5 281.6 reduce-scatter.15
  2915.6 281.6 reduce-scatter.17
  (1 shorter events, 47.2 us)
where the time goes:
time: 3210 us; the launch traced here: 3200 us
  waiting for transfers between devices  2310 us (72%)
  blocking collectives  279 us (9%)
  matrix products  231 us (7%)
  other arithmetic  194 us (6%)
  starting transfers between devices  92 us (3%)
  local copies, waits for them, and re-layouts  79.1 us (2%)
    ppermute x54, waiting for transfers between devices, shifted(): lax.ppermute(shard, axis, [(i, (i + by) % length) for i in range(length)])  438 us
    reduce_scatter x1, waiting for transfers between devices, local(): lax.psum_scatter(grad_mlp_in, 'fsdp', scatter_dimension=0, tiled=True)  286 us
    reduce_scatter x1, waiting for transfers between devices, local(): lax.psum_scatter(grad_mlp_out, 'fsdp', scatter_dimension=0, tiled=True)  286 us
    psum x4, waiting for transfers between devices, head_total(): return lax.psum(partial_value, 'tp')  250 us
    all_gather x2, waiting for transfers between devices, forward_pass(): lax.all_gather(w_mlp_in, 'fsdp', axis=0, tiled=True)  242 us
    all_gather x2, waiting for transfers between devices, forward_pass(): lax.all_gather(w_mlp_out, 'fsdp', axis=0, tiled=True)  232 us
    psum x1, waiting for transfers between devices, local(): lax.psum((contract_cols(g_q_raw, saved_pass['wq_all']), contract_cols(g_k...  105 us
    reduce_scatter x1, waiting for transfers between devices, local(): lax.psum_scatter(grad_query, 'fsdp', scatter_dimension=0, tiled=True)  92.3 us
  transfers between devices with their start and end apart: 79, of which 45 were waited for; matrix products, arithmetic and copies ran while one was open for 11% of the time, Pallas kernels for 0%

commit v1 on v0

v1 whole, which is shorter than its diff:
```python
import functools
import math

import jax
import jax.numpy as jnp
from jax import lax
from jax.experimental import pallas as pl
from jax.experimental.pallas import tpu as pltpu
from jax.sharding import PartitionSpec as P

HD = 128
ROT = 32
WAYS = 4
DEPTH = 8
SEQLEN = 2048
EPS = 1e-05
NEG = -1e30
F32 = jnp.float32
BF16 = jnp.bfloat16
VMEM_LIMIT = 56 * 2**20


def ring_order(count):
    return [2 * p if p < count // 2 else 2 * (count - 1 - p) + 1 for p in range(count)]


def ring_tables(count):
    order = ring_order(count)
    place = [0] * count
    for p, index in enumerate(order):
        place[index] = p
    return order, place


def ring_hop(value, order, base_count, by):
    size = len(order)
    pairs = []
    for start in range(0, base_count, size):
        pairs += [(start + order[p], start + order[(p + by) % size]) for p in range(size)]
    return lax.ppermute(value, "fsdp", pairs)


def swap_tp(value, bit):
    return lax.ppermute(value, "tp", [(i, i ^ bit) for i in range(lax.axis_size("tp"))])


def swap_fsdp(value, bit):
    return lax.ppermute(value, "fsdp", [(i, i ^ bit) for i in range(lax.axis_size("fsdp"))])


def after(value, *others):
    return lax.optimization_barrier((value, *others))[0]


class Ring:
    def __init__(self, size):
        self.total = lax.axis_size("fsdp")
        self.size = size
        if size == self.total:
            self.order, place = ring_tables(size)
        else:
            self.order, place = ring_tables(size)
        own = lax.axis_index("fsdp") % size
        self.own = own
        self.table = jnp.array(self.order, jnp.int32)
        self.place = jnp.array(place, jnp.int32)[own]

    def up(self, value):
        return ring_hop(value, self.order, self.total, 1)

    def down(self, value):
        return ring_hop(value, self.order, self.total, -1)

    def index(self, offset):
        return self.table[(self.place + offset) % self.size]


def ring_gather(ring, shard, start_after=()):
    rows = shard.shape[0]
    half = rows // 2
    if start_after:
        moving = after(shard, *start_after)
    else:
        moving = shard
    full = jnp.zeros((rows * ring.size,) + shard.shape[1:], shard.dtype)
    full = lax.dynamic_update_slice(full, shard, (ring.own * rows, 0))
    going_up, going_down = moving[:half], moving[half:]
    marks = []
    for step in range(1, ring.size):
        going_up, going_down = ring.up(going_up), ring.down(going_down)
        full = lax.dynamic_update_slice(full, going_up, (ring.index(-step) * rows, 0))
        full = lax.dynamic_update_slice(full, going_down, (ring.index(step) * rows + half, 0))
        marks.append((going_up, going_down))
    return full, marks


def ring_reduce(ring, rows, block):
    half = rows // 2
    going_up = going_down = None
    for step in range(1, ring.size + 1):
        up_block = block(ring.index(-step) * rows, half)
        down_block = block(ring.index(step) * rows + half, half)
        if step > 1:
            up_block = up_block + going_up.astype(F32)
            down_block = down_block + going_down.astype(F32)
        if step == ring.size:
            return jnp.concatenate([up_block, down_block], 0)
        going_up, going_down = ring.up(up_block.astype(BF16)), ring.down(down_block.astype(BF16))


def small_gather(value):
    own = lax.axis_index("fsdp")
    bit = 1
    while bit < lax.axis_size("fsdp"):
        other = swap_fsdp(value, bit)
        value = jnp.where(
            (own & bit) == 0,
            jnp.concatenate([value, other], 1),
            jnp.concatenate([other, value], 1),
        )
        bit *= 2
    return value


def small_scatter(value):
    own = lax.axis_index("fsdp")
    value = value + swap_tp(value, 1)
    value = value + swap_tp(value, 2)
    bit = lax.axis_size("fsdp") // 2
    while bit >= 1:
        width = value.shape[1] // 2
        low, high = value[:, :width], value[:, width:]
        is_low = (own & bit) == 0
        value = jnp.where(is_low, low, high) + swap_fsdp(jnp.where(is_low, high, low), bit)
        bit //= 2
    return value


def small_sum(value):
    value = value + swap_tp(value, 1)
    value = value + swap_tp(value, 2)
    bit = lax.axis_size("fsdp") // 2
    while bit >= 1:
        value = value + swap_fsdp(value, bit)
        bit //= 2
    return value


class Quarter:
    def __init__(self, tokens):
        tp_index = lax.axis_index("tp")
        self.core = tp_index % 2
        self.side = tp_index // 2
        self.half = tokens // 2
        self.rows = tokens // 4
        self.start = self.core * self.half + self.side * self.rows

    def own(self, value):
        return lax.dynamic_slice_in_dim(value, self.start, self.rows, 0)

    def total(self, product):
        away = product((1 - self.core) * self.half, self.half).astype(BF16)
        here = product(self.core * self.half, self.half)
        chip = here + swap_tp(away, 1).astype(F32)
        keep = lax.dynamic_slice_in_dim(chip, self.side * self.rows, self.rows, 0)
        send = lax.dynamic_slice_in_dim(chip, (1 - self.side) * self.rows, self.rows, 0)
        return keep + swap_tp(send.astype(BF16), 2).astype(F32)

    def gather(self, value):
        other = swap_tp(value, 2)
        half = jnp.where(
            self.side == 0,
            jnp.concatenate([value, other], 0),
            jnp.concatenate([other, value], 0),
        )
        far = swap_tp(half, 1)
        return jnp.where(
            self.core == 0,
            jnp.concatenate([half, far], 0),
            jnp.concatenate([far, half], 0),
        )


def gelu_exact(values):
    return jax.nn.gelu(values, approximate=False)


def normed(values):
    centre = values - jnp.mean(values, -1, keepdims=True)
    scale = lax.rsqrt(jnp.mean(centre * centre, -1, keepdims=True) + EPS)
    return centre * scale, scale


def norm_back(grad, gain_row, hat, scale):
    inner = grad * gain_row
    grad_values = scale * (
        inner
        - jnp.mean(inner, -1, keepdims=True)
        - hat * jnp.mean(inner * hat, -1, keepdims=True)
    )
    return grad_values, jnp.sum(grad * hat, 0)


def mix_ways(mix_rows, history_rows, way_list):
    ways = []
    for way in way_list:
        total = None
        for depth in range(DEPTH):
            column = way * DEPTH + depth
            term = mix_rows[:, column : column + 1] * history_rows[depth].astype(F32)
            total = term if total is None else total + term
        ways.append(total)
    return ways


def rope_tables(positions):
    half_rot = ROT // 2
    frequency = 10000.0 ** (-2.0 * jnp.arange(half_rot, dtype=F32) / ROT)
    angle = positions.astype(F32)[:, None] * frequency[None, :]
    cosine, sine = jnp.cos(angle), jnp.sin(angle)
    rest = HD - ROT
    count = positions.shape[0]
    straight = jnp.concatenate([cosine, cosine, jnp.ones((count, rest), F32)], 1)
    crossed = jnp.concatenate([-sine, sine, jnp.zeros((count, rest), F32)], 1)
    return straight, crossed


def rope_in_kernel(value, straight, crossed):
    half_rot = ROT // 2
    lane = lax.broadcasted_iota(jnp.int32, value.shape, 1)
    partner = jnp.where(
        lane < half_rot,
        pltpu.roll(value, HD - half_rot, 1),
        pltpu.roll(value, half_rot, 1),
    )
    return value * straight + partner * crossed


def project_kernel(q_in, k_in, v_in, wq, wk, wv, straight, crossed, q_out, k_out, v_out):
    even, odd = straight[...], crossed[...]
    heads = q_out.shape[1] // HD
    for source, weight, target in ((q_in, wq, q_out), (k_in, wk, k_out)):
        raw = jnp.dot(source[...], weight[...], preferred_element_type=F32)
        for head in range(heads):
            cut = slice(head * HD, (head + 1) * HD)
            target[:, cut] = rope_in_kernel(raw[:, cut], even, odd).astype(BF16)
    v_out[...] = jnp.dot(v_in[...], wv[...], preferred_element_type=F32).astype(BF16)


def project(q_in, k_in, v_in, wq, wk, wv, straight, crossed):
    tokens, width = q_in.shape
    columns = wq.shape[1]
    step = 2 * HD
    rows = pl.BlockSpec((tokens, width), lambda i: (0, 0))
    weight = pl.BlockSpec((width, step), lambda i: (0, i))
    table = pl.BlockSpec((tokens, HD), lambda i: (0, 0))
    out = pl.BlockSpec((tokens, step), lambda i: (0, i))
    shape = jax.ShapeDtypeStruct((tokens, columns), BF16)
    return pl.pallas_call(
        project_kernel,
        grid=(columns // step,),
        in_specs=[rows] * 3 + [weight] * 3 + [table] * 2,
        out_specs=[out] * 3,
        out_shape=[shape] * 3,
        compiler_params=pltpu.CompilerParams(vmem_limit_bytes=VMEM_LIMIT),
        cost_estimate=pl.CostEstimate(
            flops=6 * tokens * width * columns,
            bytes_accessed=6 * tokens * width + 6 * width * columns + 6 * tokens * columns,
            transcendentals=0,
        ),
        name="project",
    )(q_in, k_in, v_in, wq, wk, wv, straight, crossed)


def visible_mask(shape, query_start, first_seen):
    key_index = lax.broadcasted_iota(jnp.int32, shape, 1)
    query_index = query_start + lax.broadcasted_iota(jnp.int32, (shape[0], 1), 0)
    return (key_index <= query_index) & (key_index >= query_index - first_seen)


def attend_kernel(base, positions, q_ref, k_ref, v_ref, out_ref, low_ref, lse_ref):
    block = q_ref.shape[0]
    start = base[0] + pl.program_id(1) * block
    scores = lax.dot_general(
        q_ref[...], k_ref[...], (((1,), (1,)), ((), ())), preferred_element_type=F32
    ) * (1.0 / math.sqrt(HD))
    seen = visible_mask(scores.shape, start, positions[...])
    scores = jnp.where(seen, scores, NEG)
    top = jnp.max(scores, 1, keepdims=True)
    weights = jnp.exp(scores - top)
    total = jnp.sum(weights, 1, keepdims=True)
    mixed = jnp.dot(weights.astype(BF16), v_ref[...], preferred_element_type=F32) / total
    out_ref[...] = mixed
    low_ref[...] = mixed.astype(BF16)
    lse_ref[...] = jnp.broadcast_to(top + jnp.log(total), lse_ref.shape)


def attend(queries, keys, values, positions, base):
    tokens, columns = queries.shape
    heads = columns // HD
    length = keys.shape[0]
    block = min(128, tokens)
    q_spec = pl.BlockSpec((block, HD), lambda h, i: (i, h))
    kv_spec = pl.BlockSpec((length, HD), lambda h, i: (0, h))
    return pl.pallas_call(
        attend_kernel,
        grid=(heads, tokens // block),
        in_specs=[
            pl.BlockSpec(memory_space=pltpu.SMEM),
            pl.BlockSpec((block, 1), lambda h, i: (i, 0)),
            q_spec,
            kv_spec,
            kv_spec,
        ],
        out_specs=[q_spec, q_spec, q_spec],
        out_shape=[
            jax.ShapeDtypeStruct((tokens, columns), F32),
            jax.ShapeDtypeStruct((tokens, columns), BF16),
            jax.ShapeDtypeStruct((tokens, columns), F32),
        ],
        compiler_params=pltpu.CompilerParams(vmem_limit_bytes=VMEM_LIMIT),
        cost_estimate=pl.CostEstimate(
            flops=4 * tokens * length * columns,
            bytes_accessed=4 * length * columns + 12 * tokens * columns,
            transcendentals=tokens * length * heads,
        ),
        name="attend",
    )(base, positions, queries, keys, values)


def attend_back_kernel(
    base, positions, straight, crossed, q_ref, k_ref, v_ref, g_ref, out_ref, lse_ref,
    gq_ref, gk_ref, gv_ref,
):
    step = pl.program_id(1)
    block = q_ref.shape[0]
    scale = 1.0 / math.sqrt(HD)
    start = base[0] + step * block
    queries, keys, values, grad = q_ref[...], k_ref[...], v_ref[...], g_ref[...]
    across = (((1,), (1,)), ((), ()))
    down = (((0,), (0,)), ((), ()))
    delta = jnp.sum(grad.astype(F32) * out_ref[...], 1, keepdims=True)
    scores = lax.dot_general(queries, keys, across, preferred_element_type=F32) * scale
    seen = visible_mask(scores.shape, start, positions[...])
    probs = jnp.where(seen, jnp.exp(scores - lse_ref[:, :1]), 0.0)
    grad_probs = lax.dot_general(grad, values, across, preferred_element_type=F32)
    grad_scores = (probs * (grad_probs - delta)).astype(BF16)
    grad_query = jnp.dot(grad_scores, keys, preferred_element_type=F32) * scale
    gq_ref[...] = rope_in_kernel(grad_query, straight[...], -crossed[...]).astype(BF16)
    grad_key = lax.dot_general(grad_scores, queries, down, preferred_element_type=F32) * scale
    grad_value = lax.dot_general(probs.astype(BF16), grad, down, preferred_element_type=F32)

    @pl.when(step == 0)
    def _():
        gk_ref[...] = grad_key
        gv_ref[...] = grad_value

    @pl.when(step > 0)
    def _():
        gk_ref[...] += grad_key
        gv_ref[...] += grad_value


def attend_back(queries, keys, values, grad, out, lse, positions, base, straight, crossed):
    tokens, columns = queries.shape
    heads = columns // HD
    length = keys.shape[0]
    block = min(128, tokens)
    q_spec = pl.BlockSpec((block, HD), lambda h, i: (i, h))
    kv_spec = pl.BlockSpec((length, HD), lambda h, i: (0, h))
    table = pl.BlockSpec((block, HD), lambda h, i: (i, 0))
    return pl.pallas_call(
        attend_back_kernel,
        grid=(heads, tokens // block),
        in_specs=[
            pl.BlockSpec(memory_space=pltpu.SMEM),
            pl.BlockSpec((block, 1), lambda h, i: (i, 0)),
            table,
            table,
            q_spec,
            kv_spec,
            kv_spec,
            q_spec,
            q_spec,
            q_spec,
        ],
        out_specs=[q_spec, kv_spec, kv_spec],
        out_shape=[
            jax.ShapeDtypeStruct((tokens, columns), BF16),
            jax.ShapeDtypeStruct((length, columns), F32),
            jax.ShapeDtypeStruct((length, columns), F32),
        ],
        compiler_params=pltpu.CompilerParams(vmem_limit_bytes=VMEM_LIMIT),
        cost_estimate=pl.CostEstimate(
            flops=10 * tokens * length * columns,
            bytes_accessed=12 * length * columns + 14 * tokens * columns,
            transcendentals=tokens * length * heads,
        ),
        name="attend_back",
    )(base, positions, straight, crossed, queries, keys, values, grad, out, lse)


def turn_back_kernel(value_ref, straight, crossed, out_ref):
    for head in range(value_ref.shape[1] // HD):
        cut = slice(head * HD, (head + 1) * HD)
        out_ref[:, cut] = rope_in_kernel(
            value_ref[:, cut], straight[...], -crossed[...]
        ).astype(BF16)


def turn_back(value, straight, crossed):
    return pl.pallas_call(
        turn_back_kernel,
        out_shape=jax.ShapeDtypeStruct(value.shape, BF16),
        compiler_params=pltpu.CompilerParams(vmem_limit_bytes=VMEM_LIMIT),
        cost_estimate=pl.CostEstimate(
            flops=4 * value.size, bytes_accessed=6 * value.size, transcendentals=0
        ),
        name="turn_back",
    )(value, straight, crossed)


def dot_f32(left, right):
    return jnp.dot(left, right, preferred_element_type=F32)


def dot_cols(left, right):
    return lax.dot_general(left, right, (((1,), (1,)), ((), ())), preferred_element_type=F32)


def rows_of(left, right):
    def product(start, count):
        return dot_cols(lax.dynamic_slice_in_dim(left, start, count, 0), right)

    return product


def weight_block(left, right):
    def block(start, count):
        part = lax.dynamic_slice_in_dim(left, start, count, 1)
        return lax.dot_general(part, right, (((0,), (0,)), ((), ())), preferred_element_type=F32)

    return block


def local(
    history,
    mix_in,
    doc_positions,
    gain_q,
    gain_k,
    gain_v,
    gain_mlp,
    gain_mix,
    w_query,
    w_key,
    w_value,
    w_attn_out,
    w_mlp_in,
    w_mlp_out,
    w_mix_in,
    w_mix_out,
    out_grad,
    next_grad,
):
    tokens = history.shape[1]
    shard_rows, columns = w_query.shape
    group_size = SEQLEN // tokens
    highest = lax.Precision.HIGHEST
    ring = Ring(lax.axis_size("fsdp"))
    group = Ring(group_size)
    quarter = Quarter(tokens)

    small = jnp.concatenate(
        [jnp.stack([gain_q, gain_k, gain_v, gain_mlp, gain_mix], 0), w_mix_in.T], 0
    )
    small_all = small_gather(small).astype(F32)
    gain_rows = [small_all[i : i + 1] for i in range(5)]
    first_mix = small_all[5:]
    second_mix = w_mix_out.astype(F32)
    qk_all, qk_marks = ring_gather(ring, jnp.concatenate([w_query, w_key], 1))
    vo_all, vo_marks = ring_gather(ring, jnp.concatenate([w_value, w_attn_out], 1))
    hold = (*qk_marks[-2], *vo_marks[-2])
    wi_all, _ = ring_gather(ring, w_mlp_in, hold)
    wf_all, _ = ring_gather(ring, w_mlp_out, hold)
    wq_all, wk_all = qk_all[:, :columns], qk_all[:, columns:]
    wv_all, wo_all = vo_all[:, :columns], vo_all[:, columns:]

    ways = mix_ways(mix_in, history, range(3))
    ins = [
        (normed(way)[0] * gain_row).astype(BF16)
        for way, gain_row in zip(ways, gain_rows[:3], strict=True)
    ]
    q_in, k_in, v_in = ins
    straight, crossed = rope_tables(doc_positions)
    queries, keys, values = project(q_in, k_in, v_in, wq_all, wk_all, wv_all, straight, crossed)

    keys_all = jnp.zeros((tokens * group_size, columns), BF16)
    values_all = jnp.zeros((tokens * group_size, columns), BF16)
    keys_all = lax.dynamic_update_slice(keys_all, keys, (group.own * tokens, 0))
    values_all = lax.dynamic_update_slice(values_all, values, (group.own * tokens, 0))
    moving_keys, moving_values = keys, values
    for step in range(1, group_size):
        moving_keys, moving_values = group.up(moving_keys), group.down(moving_values)
        keys_all = lax.dynamic_update_slice(
            keys_all, moving_keys, (group.index(-step) * tokens, 0)
        )
        values_all = lax.dynamic_update_slice(
            values_all, moving_values, (group.index(step) * tokens, 0)
        )
    position_column = doc_positions[:, None]
    base = (group.own * tokens).astype(jnp.int32)[None]
    attn, attn_low, lse = attend(queries, keys_all, values_all, position_column, base)

    own_mix = quarter.own(mix_in)
    own_history = lax.dynamic_slice_in_dim(history, quarter.start, quarter.rows, 1)
    own_ways = mix_ways(own_mix, own_history, range(WAYS))
    residual = own_ways[3] + quarter.total(rows_of(attn_low, wo_all))
    res_hat, res_scale = normed(residual)
    mlp_in = quarter.gather((res_hat * gain_rows[3]).astype(BF16))

    up_proj = dot_f32(mlp_in, wi_all)
    act_rows = gelu_exact(up_proj).astype(BF16)
    block_val = residual + quarter.total(rows_of(act_rows, wf_all))

    block_hat, block_scale = normed(block_val)
    hidden_raw = lax.dot_general(
        block_hat * gain_rows[4], first_mix, (((1,), (1,)), ((), ())), precision=highest
    )
    hidden, gelu_pullback = jax.vjp(gelu_exact, hidden_raw)
    next_own = jnp.dot(hidden, second_mix, precision=highest)
    own_next_grad = quarter.own(next_grad)
    g_hidden = lax.dot_general(
        own_next_grad, second_mix, (((1,), (1,)), ((), ())), precision=highest
    )
    g_second = lax.dot_general(
        hidden, own_next_grad, (((0,), (0,)), ((), ())), precision=highest
    )
    g_hidden_raw = gelu_pullback(g_hidden)[0]
    g_mix_norm = jnp.dot(g_hidden_raw, first_mix, precision=highest)
    g_first = lax.dot_general(
        g_hidden_raw, block_hat * gain_rows[4], (((0,), (0,)), ((), ())), precision=highest
    )
    g_block_mix, g_gain_mix = norm_back(g_mix_norm, gain_rows[4], block_hat, block_scale)
    g_block = quarter.own(out_grad).astype(F32) + g_block_mix
    g_block_low = quarter.gather(g_block.astype(BF16))

    g_act = dot_f32(g_block_low, wf_all)
    g_up = jax.vjp(gelu_exact, up_proj)[1](g_act)[0].astype(BF16)
    g_mlp_in = quarter.total(rows_of(g_up, wi_all))
    grad_mlp_out = ring_reduce(ring, shard_rows, weight_block(g_block_low, act_rows))
    grad_mlp_in = ring_reduce(ring, shard_rows, weight_block(mlp_in, g_up))
    g_res_norm, g_gain_mlp = norm_back(g_mlp_in, gain_rows[3], res_hat, res_scale)
    g_res = g_block + g_res_norm
    g_res_low = quarter.gather(g_res.astype(BF16))

    g_attn = dot_f32(g_res_low, wo_all).astype(BF16)
    g_q_raw, g_keys_part, g_values_part = attend_back(
        queries, keys_all, values_all, g_attn, attn, lse, position_column, base, straight, crossed
    )
    moving_keys = moving_values = None
    for step in range(1, group_size + 1):
        key_block = lax.dynamic_slice_in_dim(
            g_keys_part, group.index(-step) * tokens, tokens, 0
        )
        value_block = lax.dynamic_slice_in_dim(
            g_values_part, group.index(step) * tokens, tokens, 0
        )
        if step > 1:
            key_block = key_block + moving_keys.astype(F32)
            value_block = value_block + moving_values.astype(F32)
        if step < group_size:
            moving_keys = group.up(key_block.astype(BF16))
            moving_values = group.down(value_block.astype(BF16))
    g_k_raw = turn_back(key_block, straight, crossed)
    g_v_raw = value_block.astype(BF16)

    grad_attn_out = ring_reduce(ring, shard_rows, weight_block(g_res_low, attn_low))
    grad_query = ring_reduce(ring, shard_rows, weight_block(q_in, g_q_raw))
    grad_key = ring_reduce(ring, shard_rows, weight_block(k_in, g_k_raw))
    grad_value = ring_reduce(ring, shard_rows, weight_block(v_in, g_v_raw))

    way_grads_own, way_gains, way_grads = [], [], []
    for index, (raw, weight) in enumerate(
        ((g_q_raw, wq_all), (g_k_raw, wk_all), (g_v_raw, wv_all))
    ):
        grad_in = quarter.total(rows_of(raw, weight))
        hat, scale = normed(own_ways[index])
        grad_way, grad_gain = norm_back(grad_in, gain_rows[index], hat, scale)
        way_grads_own.append(grad_way)
        way_gains.append(grad_gain)
        way_grads.append(quarter.gather(grad_way.astype(BF16)).astype(F32))
    way_grads_own.append(g_res)
    way_grads.append(g_res_low.astype(F32))
    history_parts = []
    for depth in range(DEPTH):
        total = None
        for way in range(WAYS):
            column = way * DEPTH + depth
            term = mix_in[:, column : column + 1] * way_grads[way]
            total = term if total is None else total + term
        history_parts.append(total.astype(BF16))
    history_grad = jnp.stack(history_parts, 0)
    mix_columns = []
    for way in range(WAYS):
        for depth in range(DEPTH):
            mix_columns.append(jnp.sum(way_grads_own[way] * own_history[depth].astype(F32), -1))
    mix_grad = quarter.gather(jnp.stack(mix_columns, 1))

    early = small_scatter(jnp.concatenate([jnp.stack([g_gain_mlp, g_gain_mix], 0), g_first], 0))
    late = small_scatter(jnp.stack(way_gains, 0))
    grad_mix_out = small_sum(g_second)
    block_out = quarter.gather(block_val.astype(BF16))
    next_mix = quarter.gather(next_own)
    return (
        block_out,
        next_mix,
        history_grad,
        mix_grad,
        late[0],
        late[1],
        late[2],
        early[0],
        early[1],
        grad_query,
        grad_key,
        grad_value,
        grad_attn_out,
        grad_mlp_in,
        grad_mlp_out,
        early[2:].T,
        grad_mix_out,
    )


def solution(mesh):
    rows, vector, weight = P("fsdp", None), P("fsdp"), P("fsdp", "tp")
    stored = P(None, "fsdp", None)
    in_specs = (
        (stored, rows) + (vector,) * 6 + (weight,) * 6 + (rows, P(), rows, rows)
    )
    out_specs = (rows, rows, stored, rows) + (vector,) * 5 + (weight,) * 6 + (rows, P())
    return jax.shard_map(local, mesh=mesh, in_specs=in_specs, out_specs=out_specs, check_vma=False)
```

time: 3210 us -> 1080 us (0.34)
  waiting for transfers between devices: 2310 us -> 389 us
  blocking collectives: 279 us -> 0 us
  starting transfers between devices: 92 us -> 198 us
  matrix products: 231 us -> 126 us
  Pallas kernels: 0 us -> 54 us
    reduce_scatter x7 -> x0, waiting for transfers between devices: 880 us -> none  [the longest x1 286 us: local(): lax.psum_scatter(grad_mlp_in, 'fsdp', scatter_dimension=0, tiled=True)]
    all_gather x12 -> x0, waiting for transfers between devices: 552 us -> none  [the longest x2 242 us: forward_pass(): lax.all_gather(w_mlp_in, 'fsdp', axis=0, tiled=True)]
    psum x6 -> x0, waiting for transfers between devices: 435 us -> none  [the longest x4 250 us: head_total(): return lax.psum(partial_value, 'tp')]
    all_gather x12 -> x0, blocking collectives: 240 us -> none  [the longest x2 61.6 us: forward_pass(): lax.all_gather(w_mix_in, 'fsdp', axis=0, tiled=True)]
    ppermute x54 -> x200, starting transfers between devices: 90.4 us -> 198 us  [the longest x152 159 us: ring_hop(): return lax.ppermute(value, 'fsdp', pairs)]
    dot_general x65 -> x117, matrix products: 231 us -> 126 us  [the longest x96 47.7 us: block(): lax.dot_general(part, right, (((0,), (0,)), ((), ())), preferred_element_...]
    reduce_sum x28 -> x21, other arithmetic: 96.6 us -> 34.1 us  [the longest x8 22.5 us: normed(): centre = values - jnp.mean(values, -1, keepdims=True)]
    unnamed x9 -> x8, other arithmetic: 25.1 us -> 79.7 us
  transfers between devices with their start and end apart: 79 -> 200, of which waited for: 45 -> 104; matrix products, arithmetic and copies ran while one was open for 11% -> 24% of each run, Pallas kernels for 0% -> 5%
where the time goes in v1:
time: 1080 us; the launch traced here: 1070 us
  waiting for transfers between devices  389 us (36%)
  starting transfers between devices  198 us (18%)
  other arithmetic  164 us (15%)
  matrix products  126 us (12%)
  local copies, waits for them, and re-layouts  102 us (9%)
  Pallas kernels  54 us (5%)
  between operations  35.3 us (3%)
    ppermute x152, waiting for transfers between devices, ring_hop(): return lax.ppermute(value, 'fsdp', pairs)  270 us
    ppermute x152, starting transfers between devices, ring_hop(): return lax.ppermute(value, 'fsdp', pairs)  159 us
    unnamed x8, other arithmetic  79.7 us
    ppermute x36, waiting for transfers between devices, swap_tp(): lax.ppermute(value, 'tp', [(i, i ^ bit) for i in range(lax.axis_size('tp'...  71.1 us
    ppermute x12, waiting for transfers between devices, swap_fsdp(): lax.ppermute(value, 'fsdp', [(i, i ^ bit) for i in range(lax.axis_size('f...  48.2 us
    dot_general x96, matrix products, block(): lax.dot_general(part, right, (((0,), (0,)), ((), ())), preferred_element_...  47.7 us
    dot_general x12, matrix products, dot_cols(): lax.dot_general(left, right, (((1,), (1,)), ((), ())), preferred_element_...  42.3 us
    dot_general x3, matrix products, dot_f32(): return jnp.dot(left, right, preferred_element_type=F32)  31.3 us
  transfers between devices with their start and end apart: 200, of which 104 were waited for; matrix products, arithmetic and copies ran while one was open for 24% of the time, Pallas kernels for 5%

profile of v1, /device:TPU:0, one launch (start us, length us, event | category | flops | bytes accessed | tf_op | source)
XLA Modules:
  0.0 1069.2 jit_solution(8203990644407763981)
XLA Ops:
  173.8 19.6 %collective-permute-done.15 = bf16[128,1024]{1,0:T(8,128)(2,1)S(1)} collective-permute-done((bf16[128,1024]{1,0:T(8,128)(2,1)S(1)}, bf16[128,1024]{1,0:T(8,128)(2,1)S(1)}, u32[]{:S(2)}, u32[]{:S(2)}) %collective-permute-start.15) | collective-permute-done | bytes 262176 | tf_op jit(solution)/shard_map/ppermute | solution.py:40
  209.0 9.1 project.1
  236.3 9.6 collective-permute-done.43
  270.0 9.6 collective-permute-done.45
  303.4 17.4 %attend.1 = (f32[512,512]{1,0:T(8,128)}, bf16[512,512]{1,0:T(8,128)(2,1)}, f32[512,512]{1,0:T(8,128)}) custom-call(s32[1]{0:T(128)} %bitcast.16.base, s32[512,1]{1,0:T(8,128)} %copy.42.positions, bf16[512,512]{1,0:T(8,128)(2,1)} %get-tuple-element.28.q_ref, bf16[2048,512]{1,0:T(8,128)(2,1)} %copy-done.37, bf16[2048,512]{1,0:T(8,128)(2,1)} %copy-done.38), custom_call_target="tpu_custom_call" | custom-call | flops 2147483648 | bytes 7340032 | tf_op jit(solution)/shard_map/attend/pallas_call | solution.py:305
  399.4 18.4 %multiply_convert_fusion = (bf16[512,2048]{1,0:T(8,128)(2,1)S(1)}, f32[512,2048]{1,0:T(8,128)}, f32[512,2048]{1,0:T(8,128)}) fusion(bf16[512,2048]{1,0:T(8,128)(2,1)S(1)} %maximum_select_fusion, bf16[2048,2048]{1,0:T(8,128)(2,1)} %constant_dynamic-update-slice_fusion.15), kind=kOutput, calls=%fused_computation.112 | convolution fusion | flops 4363124736 | bytes 20971520 | tf_op jit(solution)/shard_map/dot_general | solution.py:424
  435.5 11.5 %collective-permute-done.70 = bf16[128,2048]{1,0:T(8,128)(2,1)S(1)} collective-permute-done((bf16[128,2048]{1,0:T(8,128)(2,1)S(1)}, bf16[128,2048]{1,0:T(8,128)(2,1)S(1)}, u32[]{:S(2)}, u32[]{:S(2)}) %collective-permute-start.70) | collective-permute-done | bytes 524320 | tf_op jit(solution)/shard_map/ppermute | solution.py:44
  455.7 10.2 collective-permute-done.75
  491.1 9.2 add_convert_fusion
  580.8 16.3 %collective-permute-done.108 = f32[38,1024]{1,0:T(8,128)S(1)} collective-permute-done((f32[38,1024]{1,0:T(8,128)S(1)}, f32[38,1024]{1,0:T(8,128)S(1)}, u32[]{:S(2)}, u32[]{:S(2)}) %collective-permute-start.108) | collective-permute-done | bytes 155680 | tf_op jit(solution)/shard_map/ppermute | solution.py:48
  602.9 11.3 %collective-permute-done.109 = f32[38,512]{1,0:T(8,128)S(1)} collective-permute-done((f32[38,512]{1,0:T(8,128)S(1)}, f32[38,512]{1,0:T(8,128)S(1)}, u32[]{:S(2)}, u32[]{:S(2)}) %collective-permute-start.109) | collective-permute-done | bytes 77856 | tf_op jit(solution)/shard_map/ppermute | solution.py:48
  616.8 11.2 %collective-permute-done.110 = f32[38,256]{1,0:T(8,128)S(1)} collective-permute-done((f32[38,256]{1,0:T(8,128)S(1)}, f32[38,256]{1,0:T(8,128)S(1)}, u32[]{:S(2)}, u32[]{:S(2)}) %collective-permute-start.110) | collective-permute-done | bytes 38944 | tf_op jit(solution)/shard_map/ppermute | solution.py:48
  652.3 24.8 %attend_back.1 = (bf16[512,512]{1,0:T(8,128)(2,1)}, f32[2048,512]{1,0:T(8,128)}, f32[2048,512]{1,0:T(8,128)}) custom-call(s32[1]{0:T(128)} %bitcast.16.base, s32[512,1]{1,0:T(8,128)} %copy.42.positions, f32[512,128]{1,0:T(8,128)} %get-tuple-element.251.straight, f32[512,128]{1,0:T(8,128)} %get-tuple-element.252.crossed, ...), custom_call_target="tpu_custom_call" | custom-call | flops 5368709120 | bytes 16252928 | tf_op jit(solution)/shard_map/attend_back/pallas_call | solution.py:372
  700.9 11.5 %collective-permute-done.154 = bf16[128,512]{1,0:T(8,128)(2,1)S(1)} collective-permute-done((bf16[128,512]{1,0:T(8,128)(2,1)S(1)}, bf16[128,512]{1,0:T(8,128)(2,1)S(1)}, u32[]{:S(2)}, u32[]{:S(2)}) %collective-permute-start.154) | collective-permute-done | bytes 131104 | tf_op jit(solution)/shard_map/ppermute | solution.py:40
  754.8 9.4 collective-permute-done.156
  952.3 9.5 collective-permute-done.90
  977.2 10.7 fusion.90
  988.0 11.4 %fusion.89 = bf16[8,512,2048]{2,1,0:T(8,128)(2,1)} fusion(bf16[8,512,2048]{2,1,0:T(8,128)(2,1)} %fusion.90, f32[512]{0:T(512)S(1)} %bitcast.718, f32[512]{0:T(512)S(1)} %bitcast.686, f32[512]{0:T(512)S(1)} %bitcast.706, f32[512]{0:T(512)S(1)} %bitcast.708, bf16[1,256,2048]{2,1,0:T(8,128)(2,1)S(1)} %bitcast.572, bf16[1,256,2048]{2,1,0:T(8,128)(2,1)S(1)} %bitcast.580, ...), kind=kLoop, calls=%fused_computation.270 | loop fusion | flops 50331648 | bytes 10493953
  999.4 11.6 %fusion.88 = bf16[8,512,2048]{2,1,0:T(8,128)(2,1)} fusion(bf16[8,512,2048]{2,1,0:T(8,128)(2,1)} %fusion.89, f32[512]{0:T(512)S(1)} %bitcast.717, f32[512]{0:T(512)S(1)} %bitcast.684, f32[512]{0:T(512)S(1)} %bitcast.702, f32[512]{0:T(512)S(1)} %bitcast.704, bf16[1,256,2048]{2,1,0:T(8,128)(2,1)S(1)} %bitcast.573, bf16[1,256,2048]{2,1,0:T(8,128)(2,1)S(1)} %bitcast.581, ...), kind=kLoop, calls=%fused_computation.269 | loop fusion | flops 50331648 | bytes 10493953
  1011.1 11.4 %fusion.87 = bf16[8,512,2048]{2,1,0:T(8,128)(2,1)} fusion(bf16[8,512,2048]{2,1,0:T(8,128)(2,1)} %fusion.88, f32[512]{0:T(512)S(1)} %bitcast.716, f32[512]{0:T(512)S(1)} %bitcast.682, f32[512]{0:T(512)S(1)} %bitcast.698, f32[512]{0:T(512)S(1)} %bitcast.700, bf16[1,256,2048]{2,1,0:T(8,128)(2,1)S(1)} %bitcast.574, bf16[1,256,2048]{2,1,0:T(8,128)(2,1)S(1)} %bitcast.582, ...), kind=kLoop, calls=%fused_computation.268 | loop fusion | flops 50331648 | bytes 10493953
  1022.6 11.4 %fusion.86 = bf16[8,512,2048]{2,1,0:T(8,128)(2,1)} fusion(bf16[8,512,2048]{2,1,0:T(8,128)(2,1)} %fusion.87, f32[512]{0:T(512)S(1)} %bitcast.715, f32[512]{0:T(512)S(1)} %bitcast.678, f32[512]{0:T(512)S(1)} %bitcast.680, f32[512]{0:T(512)S(1)} %bitcast.696, bf16[1,256,2048]{2,1,0:T(8,128)(2,1)S(1)} %bitcast.575, bf16[1,256,2048]{2,1,0:T(8,128)(2,1)S(1)} %bitcast.583, ...), kind=kLoop, calls=%fused_computation.267 | loop fusion | flops 50331648 | bytes 10493953
  1034.1 11.4 %fusion.85 = bf16[8,512,2048]{2,1,0:T(8,128)(2,1)} fusion(bf16[8,512,2048]{2,1,0:T(8,128)(2,1)} %fusion.86, f32[512]{0:T(512)S(1)} %bitcast.714, f32[512]{0:T(512)S(1)} %bitcast.674, f32[512]{0:T(512)S(1)} %bitcast.676, f32[512]{0:T(512)S(1)} %bitcast.694, bf16[1,256,2048]{2,1,0:T(8,128)(2,1)S(1)} %bitcast.576, bf16[1,256,2048]{2,1,0:T(8,128)(2,1)S(1)} %bitcast.584, ...), kind=kLoop, calls=%fused_computation.266 | loop fusion | flops 50331648 | bytes 10493953
  1045.6 11.7 %fusion.84 = bf16[8,512,2048]{2,1,0:T(8,128)(2,1)} fusion(bf16[8,512,2048]{2,1,0:T(8,128)(2,1)} %fusion.85, f32[512]{0:T(512)S(1)} %bitcast.721, f32[512]{0:T(512)S(1)} %bitcast.670, f32[512]{0:T(512)S(1)} %bitcast.672, f32[512]{0:T(512)S(1)} %bitcast.692, bf16[1,256,2048]{2,1,0:T(8,128)(2,1)S(1)} %bitcast.577, bf16[1,256,2048]{2,1,0:T(8,128)(2,1)S(1)} %bitcast.585, ...), kind=kLoop, calls=%fused_computation.265 | loop fusion | flops 50331648 | bytes 10493953
  1057.3 11.4 %fusion.83 = bf16[8,512,2048]{2,1,0:T(8,128)(2,1)} fusion(bf16[8,512,2048]{2,1,0:T(8,128)(2,1)} %fusion.84, f32[512]{0:T(512)S(1)} %bitcast.713, f32[512]{0:T(512)S(1)} %bitcast.666, f32[512]{0:T(512)S(1)} %bitcast.668, f32[512]{0:T(512)S(1)} %bitcast.690, bf16[1,256,2048]{2,1,0:T(8,128)(2,1)S(1)} %bitcast.578, bf16[1,256,2048]{2,1,0:T(8,128)(2,1)S(1)} %bitcast.586, ...), kind=kLoop, calls=%fused_computation.264 | loop fusion | flops 50331648 | bytes 10493953 | tf_op jit(solution)/shard_map/stack | solution.py:603
  (992 shorter events, 734.2 us)
Async XLA Ops:
  3.6 103.7 %collective-permute-start.3 = (bf16[128,1024]{1,0:T(8,128)(2,1)}, bf16[128,1024]{1,0:T(8,128)(2,1)}, u32[]{:S(2)}, u32[]{:S(2)}) collective-permute-start(bf16[128,1024]{1,0:T(8,128)(2,1)} %get-tuple-element.143), channel_id=1, source_target_pairs={{0,8},{8,16},{16,24},{24,28},{28,20},{20,12},{12,4},{4,0},{1,9},{9... | collective-permute-start | bytes 786440 | tf_op jit(solution)/shard_map/ppermute | solution.py:40
  6.6 100.7 %collective-permute-start.4 = (bf16[128,1024]{1,0:T(8,128)(2,1)}, bf16[128,1024]{1,0:T(8,128)(2,1)S(1)}, u32[]{:S(2)}, u32[]{:S(2)}) collective-permute-start(bf16[128,1024]{1,0:T(8,128)(2,1)} %get-tuple-element.142), channel_id=1, source_target_pairs={{0,4},{8,0},{16,8},{24,16},{28,24},{20,28},{12,20},{4,12},{1,5},{9... | collective-permute-start | bytes 786440 | tf_op jit(solution)/shard_map/ppermute | solution.py:40
  9.4 99.9 %collective-permute-start.17 = (bf16[128,1024]{1,0:T(8,128)(2,1)}, bf16[128,1024]{1,0:T(8,128)(2,1)}, u32[]{:S(2)}, u32[]{:S(2)}) collective-permute-start(bf16[128,1024]{1,0:T(8,128)(2,1)} %get-tuple-element.145), channel_id=1, source_target_pairs={{0,8},{8,16},{16,24},{24,28},{28,20},{20,12},{12,4},{4,0},{1,9},{9... | collective-permute-start | bytes 786440 | tf_op jit(solution)/shard_map/ppermute | solution.py:40
  11.5 98.2 %collective-permute-start.18 = (bf16[128,1024]{1,0:T(8,128)(2,1)}, bf16[128,1024]{1,0:T(8,128)(2,1)S(1)}, u32[]{:S(2)}, u32[]{:S(2)}) collective-permute-start(bf16[128,1024]{1,0:T(8,128)(2,1)} %get-tuple-element.144), channel_id=1, source_target_pairs={{0,4},{8,0},{16,8},{24,16},{28,24},{20,28},{12,20},{4,12},{1,5},{9... | collective-permute-start | bytes 786440 | tf_op jit(solution)/shard_map/ppermute | solution.py:40
  11.7 47.1 %collective-permute-start = (bf16[41,256]{1,0:T(8,128)(2,1)S(1)}, bf16[41,256]{1,0:T(8,128)(2,1)S(1)}, u32[]{:S(2)}, u32[]{:S(2)}) collective-permute-start(bf16[41,256]{1,0:T(8,128)(2,1)S(1)} %concatenate.534), channel_id=1, source_target_pairs={{0,4},{4,0},{8,12},{12,8},{16,20},{20,16},{24,28},{28,24},{1,5},{5... | collective-permute-start | bytes 62984 | tf_op jit(solution)/shard_map/ppermute | solution.py:48
  164.2 55.5 %collective-permute-start.41 = (bf16[128,2048]{1,0:T(8,128)(2,1)}, bf16[128,2048]{1,0:T(8,128)(2,1)S(1)}, u32[]{:S(2)}, u32[]{:S(2)}) collective-permute-start(bf16[128,2048]{1,0:T(8,128)(2,1)} %get-tuple-element.139), channel_id=1, source_target_pairs={{0,8},{8,16},{16,24},{24,28},{28,20},{20,12},{12,4},{4,0},{1,9},{9... | collective-permute-start | bytes 1572872 | tf_op jit(solution)/shard_map/ppermute | solution.py:40
  166.0 56.5 %collective-permute-start.42 = (bf16[128,2048]{1,0:T(8,128)(2,1)S(1)}, bf16[128,2048]{1,0:T(8,128)(2,1)S(1)}, u32[]{:S(2)}, u32[]{:S(2)}) collective-permute-start(bf16[128,2048]{1,0:T(8,128)(2,1)S(1)} %get-tuple-element.138), channel_id=1, source_target_pairs={{0,4},{8,0},{16,8},{24,16},{28,24},{20,28},{12,20},{4,12},{1,5},{9... | collective-permute-start | bytes 1572872 | tf_op jit(solution)/shard_map/ppermute | solution.py:40
  167.1 56.4 %collective-permute-start.55 = (bf16[128,2048]{1,0:T(8,128)(2,1)}, bf16[128,2048]{1,0:T(8,128)(2,1)S(1)}, u32[]{:S(2)}, u32[]{:S(2)}) collective-permute-start(bf16[128,2048]{1,0:T(8,128)(2,1)} %get-tuple-element.141), channel_id=1, source_target_pairs={{0,8},{8,16},{16,24},{24,28},{28,20},{20,12},{12,4},{4,0},{1,9},{9... | collective-permute-start | bytes 1572872 | tf_op jit(solution)/shard_map/ppermute | solution.py:40
  282.3 41.0 %collective-permute-start.47 = (bf16[128,2048]{1,0:T(8,128)(2,1)S(1)}, bf16[128,2048]{1,0:T(8,128)(2,1)}, u32[]{:S(2)}, u32[]{:S(2)}) collective-permute-start(bf16[128,2048]{1,0:T(8,128)(2,1)S(1)} %collective-permute-done.45), channel_id=1, source_target_pairs={{0,8},{8,16},{16,24},{24,28},{28,20},{20,12},{12,4},{4,0},{1,9},{9... | collective-permute-start | bytes 1572872 | tf_op jit(solution)/shard_map/ppermute | solution.py:40
  569.6 44.6 %collective-permute-start.177 = (bf16[128,2048]{1,0:T(8,128)(2,1)S(1)}, bf16[128,2048]{1,0:T(8,128)(2,1)S(1)}, u32[]{:S(2)}, u32[]{:S(2)}) collective-permute-start(bf16[128,2048]{1,0:T(8,128)(2,1)S(1)} %fusion.68), channel_id=1, source_target_pairs={{0,4},{8,0},{16,8},{24,16},{28,24},{20,28},{12,20},{4,12},{1,5},{9... | collective-permute-start | bytes 1572872 | tf_op jit(solution)/shard_map/ppermute | solution.py:40
  571.9 72.3 %collective-permute-start.80 = (bf16[256,2048]{1,0:T(8,128)(2,1)S(1)}, bf16[256,2048]{1,0:T(8,128)(2,1)S(1)}, u32[]{:S(2)}, u32[]{:S(2)}) collective-permute-start(bf16[256,2048]{1,0:T(8,128)(2,1)S(1)} %maximum_select_fusion.11), channel_id=1, source_target_pairs={{0,1},{1,0},{2,3},{3,2},{4,5},{5,4},{6,7},{7,6},{8,9},{9,8},{10,11... | collective-permute-start | bytes 3145736 | tf_op jit(solution)/shard_map/ppermute | solution.py:44
  577.6 51.7 %collective-permute-start.185 = (bf16[128,2048]{1,0:T(8,128)(2,1)S(1)}, bf16[128,2048]{1,0:T(8,128)(2,1)S(1)}, u32[]{:S(2)}, u32[]{:S(2)}) collective-permute-start(bf16[128,2048]{1,0:T(8,128)(2,1)S(1)} %fusion.73), channel_id=1, source_target_pairs={{0,8},{8,16},{16,24},{24,28},{28,20},{20,12},{12,4},{4,0},{1,9},{9... | collective-permute-start | bytes 1572872 | tf_op jit(solution)/shard_map/ppermute | solution.py:40
  630.5 53.3 %collective-permute-start.186 = (bf16[128,2048]{1,0:T(8,128)(2,1)}, bf16[128,2048]{1,0:T(8,128)(2,1)S(1)}, u32[]{:S(2)}, u32[]{:S(2)}) collective-permute-start(bf16[128,2048]{1,0:T(8,128)(2,1)} %fusion.72), channel_id=1, source_target_pairs={{0,8},{8,16},{16,24},{24,28},{28,20},{20,12},{12,4},{4,0},{1,9},{9... | collective-permute-start | bytes 1572872 | tf_op jit(solution)/shard_map/ppermute | solution.py:40
  633.8 51.5 %collective-permute-start.193 = (bf16[128,2048]{1,0:T(8,128)(2,1)}, bf16[128,2048]{1,0:T(8,128)(2,1)}, u32[]{:S(2)}, u32[]{:S(2)}) collective-permute-start(bf16[128,2048]{1,0:T(8,128)(2,1)} %fusion.78), channel_id=1, source_target_pairs={{0,4},{8,0},{16,8},{24,16},{28,24},{20,28},{12,20},{4,12},{1,5},{9... | collective-permute-start | bytes 1572872 | tf_op jit(solution)/shard_map/ppermute | solution.py:40
  635.4 51.7 %collective-permute-start.172 = (bf16[128,2048]{1,0:T(8,128)(2,1)}, bf16[128,2048]{1,0:T(8,128)(2,1)}, u32[]{:S(2)}, u32[]{:S(2)}) collective-permute-start(bf16[128,2048]{1,0:T(8,128)(2,1)} %fusion.60), channel_id=1, source_target_pairs={{0,8},{8,16},{16,24},{24,28},{28,20},{20,12},{12,4},{4,0},{1,9},{9... | collective-permute-start | bytes 1572872 | tf_op jit(solution)/shard_map/ppermute | solution.py:40
  644.2 46.6 %collective-permute-start.179 = (bf16[128,2048]{1,0:T(8,128)(2,1)}, bf16[128,2048]{1,0:T(8,128)(2,1)}, u32[]{:S(2)}, u32[]{:S(2)}) collective-permute-start(bf16[128,2048]{1,0:T(8,128)(2,1)} %fusion.66), channel_id=1, source_target_pairs={{0,4},{8,0},{16,8},{24,16},{28,24},{20,28},{12,20},{4,12},{1,5},{9... | collective-permute-start | bytes 1572872 | tf_op jit(solution)/shard_map/ppermute | solution.py:40
  650.3 44.0 %collective-permute-start.153 = (bf16[128,512]{1,0:T(8,128)(2,1)}, bf16[128,512]{1,0:T(8,128)(2,1)S(1)}, u32[]{:S(2)}, u32[]{:S(2)}) collective-permute-start(bf16[128,512]{1,0:T(8,128)(2,1)} %convolution_convert_fusion.11), channel_id=1, source_target_pairs={{0,8},{8,16},{16,24},{24,28},{28,20},{20,12},{12,4},{4,0},{1,9},{9... | collective-permute-start | bytes 393224 | tf_op jit(solution)/shard_map/ppermute | solution.py:40
  685.3 66.8 %collective-permute-start.92 = (bf16[512,512]{1,0:T(8,128)(2,1)S(1)}, bf16[512,512]{1,0:T(8,128)(2,1)S(1)}, u32[]{:S(2)}, u32[]{:S(2)}) collective-permute-start(bf16[512,512]{1,0:T(8,128)(2,1)S(1)} %dynamic-slice_convert_fusion.1), channel_id=1, source_target_pairs={{0,4},{8,0},{12,8},{4,12},{16,20},{24,16},{28,24},{20,28},{1,5},{9... | collective-permute-start | bytes 1572872 | tf_op jit(solution)/shard_map/ppermute | solution.py:40
  687.1 65.6 %collective-permute-start.85 = (bf16[512,512]{1,0:T(8,128)(2,1)S(1)}, bf16[512,512]{1,0:T(8,128)(2,1)S(1)}, u32[]{:S(2)}, u32[]{:S(2)}) collective-permute-start(bf16[512,512]{1,0:T(8,128)(2,1)S(1)} %dynamic-slice_convert_fusion.3), channel_id=1, source_target_pairs={{0,8},{8,12},{12,4},{4,0},{16,24},{24,28},{28,20},{20,16},{1,9},{9... | collective-permute-start | bytes 1572872 | tf_op jit(solution)/shard_map/ppermute | solution.py:40
  694.8 138.0 %collective-permute-start.81 = (bf16[256,2048]{1,0:T(8,128)(2,1)S(1)}, bf16[256,2048]{1,0:T(8,128)(2,1)S(1)}, u32[]{:S(2)}, u32[]{:S(2)}) collective-permute-start(bf16[256,2048]{1,0:T(8,128)(2,1)S(1)} %convolution_convert_fusion.2), channel_id=1, source_target_pairs={{0,1},{1,0},{2,3},{3,2},{4,5},{5,4},{6,7},{7,6},{8,9},{9,8},{10,11... | collective-permute-start | bytes 3145736 | tf_op jit(solution)/shard_map/ppermute | solution.py:44
  698.0 84.4 %collective-permute-start.187 = (bf16[128,2048]{1,0:T(8,128)(2,1)S(1)}, bf16[128,2048]{1,0:T(8,128)(2,1)S(1)}, u32[]{:S(2)}, u32[]{:S(2)}) collective-permute-start(bf16[128,2048]{1,0:T(8,128)(2,1)S(1)} %fusion.71), channel_id=1, source_target_pairs={{0,8},{8,16},{16,24},{24,28},{28,20},{20,12},{12,4},{4,0},{1,9},{9... | collective-permute-start | bytes 1572872 | tf_op jit(solution)/shard_map/ppermute | solution.py:40
  788.8 41.5 %collective-permute-start.93 = (bf16[512,512]{1,0:T(8,128)(2,1)S(1)}, bf16[512,512]{1,0:T(8,128)(2,1)S(1)}, u32[]{:S(2)}, u32[]{:S(2)}) collective-permute-start(bf16[512,512]{1,0:T(8,128)(2,1)S(1)} %add_convert_fusion.3), channel_id=1, source_target_pairs={{0,4},{8,0},{12,8},{4,12},{16,20},{24,16},{28,24},{20,28},{1,5},{9... | collective-permute-start | bytes 1572872 | tf_op jit(solution)/shard_map/ppermute | solution.py:40
  856.8 48.5 %collective-permute-start.95 = (bf16[256,2048]{1,0:T(8,128)(2,1)S(1)}, bf16[256,2048]{1,0:T(8,128)(2,1)S(1)}, u32[]{:S(2)}, u32[]{:S(2)}) collective-permute-start(bf16[256,2048]{1,0:T(8,128)(2,1)S(1)} %convolution_convert_fusion), channel_id=1, source_target_pairs={{0,1},{1,0},{2,3},{3,2},{4,5},{5,4},{6,7},{7,6},{8,9},{9,8},{10,11... | collective-permute-start | bytes 3145736 | tf_op jit(solution)/shard_map/ppermute | solution.py:44
  857.4 51.9 %collective-permute-start.88 = (bf16[256,2048]{1,0:T(8,128)(2,1)S(1)}, bf16[256,2048]{1,0:T(8,128)(2,1)S(1)}, u32[]{:S(2)}, u32[]{:S(2)}) collective-permute-start(bf16[256,2048]{1,0:T(8,128)(2,1)S(1)} %convolution_convert_fusion.1), channel_id=1, source_target_pairs={{0,1},{1,0},{2,3},{3,2},{4,5},{5,4},{6,7},{7,6},{8,9},{9,8},{10,11... | collective-permute-start | bytes 3145736 | tf_op jit(solution)/shard_map/ppermute | solution.py:44
  (307 other events, 4937.0 us)
